TPU v7x, 32 devices: a whole 2x2x4 slice. The times are simulated.
32 devices in a mesh: groups: 2 (over y), ctx: 16 (over z, x, core).
Axes of the slice: x: 2, y: 2, z: 4, core: 2. Of those that a mesh axis runs over, the one named last changes fastest.
Arguments:
- queries: bfloat16 [32, 8192], P(('groups', 'ctx')), parts along dimension 0, may hold values from -120 to 120
- fresh_keys: bfloat16 [32, 512], P(('groups', 'ctx')), parts along dimension 0, may hold values from -4 to 4
- fresh_values: bfloat16 [32, 512], P(('groups', 'ctx')), parts along dimension 0, may hold values from -4 to 4
- cache_keys: bfloat16 [32768, 512], P(('groups', 'ctx')), parts along dimension 0, may hold values from -4 to 4
- stored_values: bfloat16 [32768, 512], P(('groups', 'ctx')), parts along dimension 0, may hold values from -4 to 4
- cache_lengths: int32 [32], P(('groups', 'ctx')), parts along dimension 0, may hold values from 1 to 1024, as said below
- positions: int32 [32], P('groups'), parts along dimension 0, may hold values from 0 to 15, each once
Outputs:
- attended: bfloat16 [32, 8192], P(('groups', 'ctx')), parts along dimension 0
There are 2 independent parts, one for each index of `groups`. A program takes and returns all parts, laid end to end along the dimension named above; each array names one. Nothing has to cross between parts.
Inputs may be any that keep to these rules, and one draw needn't show every extreme that they name: `cache_lengths`: each entry lies between 1 and 1024, and one shard has all 1024 slots live.
All inputs are finite; a program needn't handle non-finite values.
Results may differ from a plain program's by a relative error of at most 0.003.
Values may be sent and summed in bfloat16 or wider, within the bound.
A program may use at most 128 MiB of HBM per device.

v0:
```python
import jax
import jax.numpy as jnp
from jax import lax
from jax.sharding import PartitionSpec as P

HEADS_PER_GROUP = 16
HEAD_WIDTH = 128


def body(queries, fresh_keys, fresh_values, cache_keys, stored_values, cache_lengths, positions):
    device_rank = lax.axis_index("ctx")
    new_rows = fresh_keys.shape[0]
    cache_rows = cache_keys.shape[0]
    head_size = HEAD_WIDTH
    group_size = HEADS_PER_GROUP
    kv_heads = fresh_keys.shape[1] // head_size
    query_heads = kv_heads * group_size
    all_keys = jnp.concatenate([cache_keys, fresh_keys], axis=0)
    all_values = jnp.concatenate([stored_values, fresh_values], axis=0)
    gathered = lax.all_gather(queries, "ctx", axis=0, tiled=True)
    total_new = gathered.shape[0]
    key_order = lax.dynamic_slice_in_dim(positions, device_rank * new_rows, new_rows, 0)
    live = jnp.arange(cache_rows, dtype=jnp.int32) < cache_lengths[0]
    cache_seen = jnp.broadcast_to(live[None, :], (total_new, cache_rows))
    new_seen = key_order[None, :] <= positions[:, None]
    visible = jnp.concatenate([cache_seen, new_seen], axis=1)
    maxima_list = []
    totals_list = []
    sums_list = []
    for head_group in range(kv_heads):
        query_part = gathered[
            :, head_group * group_size * head_size : (head_group + 1) * group_size * head_size
        ].reshape(total_new, group_size, head_size)
        key_part = all_keys[:, head_group * head_size : (head_group + 1) * head_size]
        value_part = all_values[:, head_group * head_size : (head_group + 1) * head_size]
        scores = jnp.einsum(
            "ngd,kd->ngk", query_part, key_part, preferred_element_type=jnp.float32
        ) * head_size ** (-0.5)
        scores = jnp.where(visible[:, None, :], scores, -jnp.inf)
        maxima = jnp.max(scores, axis=-1)
        weights = jnp.exp(scores - maxima[..., None]).astype(jnp.bfloat16)
        totals = jnp.sum(weights.astype(jnp.float32), axis=-1)
        sums = jnp.einsum("ngk,kd->ngd", weights, value_part, preferred_element_type=jnp.float32)
        maxima_list.append(maxima)
        totals_list.append(totals)
        sums_list.append(sums.reshape(total_new, group_size * head_size))
    block_max = jnp.concatenate(maxima_list, axis=1)
    block_total = jnp.concatenate(totals_list, axis=1)
    block_sum = jnp.concatenate(sums_list, axis=1)
    sums_in, maxima_in, totals_in = (
        lax.all_to_all(block_sum[None], "ctx", split_axis=1, concat_axis=0, tiled=True),
        lax.all_to_all(block_max[None], "ctx", split_axis=1, concat_axis=0, tiled=True),
        lax.all_to_all(block_total[None], "ctx", split_axis=1, concat_axis=0, tiled=True),
    )
    overall = jnp.max(maxima_in, axis=0)
    scale = jnp.exp(maxima_in - overall[None])
    sources = sums_in.shape[0]
    numerator = jnp.sum(
        sums_in.reshape(sources, new_rows, query_heads, head_size) * scale[..., None], axis=0
    )
    denominator = jnp.sum(totals_in * scale, axis=0)
    result = numerator / denominator[..., None]
    return result.reshape(new_rows, query_heads * head_size).astype(jnp.bfloat16)


def solution(mesh):
    return jax.shard_map(
        body,
        mesh=mesh,
        in_specs=(
            P(("groups", "ctx"), None),
            P(("groups", "ctx"), None),
            P(("groups", "ctx"), None),
            P(("groups", "ctx"), None),
            P(("groups", "ctx"), None),
            P(("groups", "ctx")),
            P("groups"),
        ),
        out_specs=P(("groups", "ctx"), None),
        check_vma=False,
    )
```

profile of v0, /device:TPU:0, one launch (start us, length us, event | category | flops | bytes accessed | tf_op | source)
XLA Modules:
  0.0 74.4 jit_solution(8473984056943046898)
XLA Ops:
  0.7 1.2 %dynamic_slice.3 = s32[1]{0:T(128)} dynamic-slice(s32[16]{0:T(128)} %param.13, s32[]{:T(128)S(6)} %select_n.16), dynamic_slice_sizes={1} | dynamic-slice | bytes 12 | tf_op jit(solution)/shard_map/dynamic_slice | solution.py:22
  1.9 1.3 %compare_bitcast_fusion = pred[16,1]{0,1:T(4,128)(4,1)S(1)} fusion(s32[16]{0:T(128)} %param.13, s32[]{:T(128)} %bitcast.1), kind=kLoop, calls=%fused_computation.57 | loop fusion | flops 16 | bytes 84 | tf_op jit(solution)/shard_map/le | solution.py:25
  3.2 0.1 copy.10
  3.3 0.0 copy-start.1
  3.3 24.9 %all-gather = bf16[16,1,8192]{2,1,0:T(2,128)(2,1)S(1)} all-gather(bf16[1,1,8192]{2,1,0:T(2,128)(2,1)} %bitcast.115), channel_id=1, replica_groups=mesh['groups'=2,'ctx'=16] {'ctx'}, dimensions={0}, use_global_device_ids=true | all-gather | bytes 278528 | tf_op jit(solution)/shard_map/all_gather | solution.py:20
  28.2 0.3 copy.25
  28.6 0.0 copy-start.6
  28.7 0.0 copy-done.1
  28.7 0.1 constant_dynamic-update-slice_fusion.1
  28.8 0.5 copy-done.6
  29.3 0.4 fusion.15
  29.7 0.4 fusion.16
  30.2 0.0 copy-start.2
  30.2 0.4 fusion.17
  30.6 1.4 %fusion.18 = (f32[16,16]{1,0:T(8,128)S(1)}, f32[16,16,1025]{2,1,0:T(8,128)}) fusion(bf16[16,16,128]{2,1,0:T(8,128)(2,1)S(1)} %bitcast.105, bf16[1025,512]{1,0:T(8,128)(2,1)S(1)} %constant_dynamic-update-slice_fusion, pred[16,1025]{1,0:T(8,128)(4,1)S(1)} %pad_add_fusion), kind=kOutput, calls=%fused_computation.61 | convolution fusion | flops 67961344 | bytes 1398784 | tf_op jit(solution)/shard_map/ngd,kd->ngk/dot_general | solution.py:36
  32.0 0.0 copy-start.4
  32.0 0.0 copy-done.2
  32.0 0.7 pad_maximum_fusion.1
  32.6 0.0 copy-done.4
  32.6 4.1 %all-to-all-start.1 = ((f32[1,16,64]{2,0,1:T(1,128)}), f32[1,16,64]{2,0,1:T(1,128)}, u32[]{:S(2)}, u32[]{:S(2)}) async-start(f32[1,16,64]{2,0,1:T(1,128)} %bitcast.116), calls=%async_computation.1 | async-start | bytes 16384 | tf_op jit(solution)/shard_map/all_to_all | solution.py:52
  36.7 0.0 copy-start.7
  36.7 1.3 %constant_dynamic-update-slice_fusion.3 = bf16[1025,512]{1,0:T(8,128)(2,1)S(1)} fusion(bf16[1024,512]{1,0:T(8,128)(2,1)} %param.11), kind=kLoop, calls=%fused_computation.48 | loop fusion | bytes 2097152
  38.0 0.0 copy-done.7
  38.1 0.0 copy-start.3
  38.1 0.4 fusion.8
  38.5 0.3 copy-done.3
  38.8 0.5 convert_reduce_fusion
  39.2 0.0 copy-start
  39.2 0.0 copy-start.5
  39.2 0.4 fusion.9
  39.6 0.9 %copy-done = f32[16,16,1025]{2,1,0:T(8,128)S(1)} copy-done((f32[16,16,1025]{2,1,0:T(8,128)S(1)}, f32[16,16,1025]{2,1,0:T(8,128)}, u32[]{:S(2)}) %copy-start) | copy-done | bytes 1049624
  40.5 0.0 copy-done.5
  40.5 0.4 fusion.11
  40.9 0.5 convert_reduce_fusion.2
  41.4 0.4 fusion.10
  41.7 0.1 copy_bitcast_fusion.1
  41.8 0.1 copy_bitcast_fusion.3
  41.9 0.7 pad_maximum_fusion.2
  42.6 0.6 all-to-all-done.1
  43.2 5.4 %all-to-all-start.2 = ((f32[1,16,64]{2,0,1:T(1,128)}), f32[1,16,64]{2,0,1:T(1,128)S(1)}, u32[]{:S(2)}, u32[]{:S(2)}) async-start(f32[1,16,64]{2,0,1:T(1,128)} %bitcast.20), calls=%async_computation.2 | async-start | bytes 16384 | tf_op jit(solution)/shard_map/all_to_all | solution.py:53
  48.6 1.3 %broadcast_in_dim.55 = f32[1,16,8192]{2,0,1:T(1,128)} reshape(f32[16,8192]{1,0:T(8,128)S(1)} %pad_maximum_fusion) | data formatting | bytes 1048576 | tf_op jit(solution)/shard_map/broadcast_in_dim | solution.py:51
  49.9 5.0 %all-to-all-done.2 = f32[1,16,64]{2,0,1:T(1,128)S(1)} async-done(((f32[1,16,64]{2,0,1:T(1,128)}), f32[1,16,64]{2,0,1:T(1,128)S(1)}, u32[]{:S(2)}, u32[]{:S(2)}) %all-to-all-start.2) | async-done | bytes 4128 | tf_op jit(solution)/shard_map/all_to_all | solution.py:53
  54.9 3.6 %all-to-all-start = ((f32[1,16,8192]{2,0,1:T(1,128)}), f32[1,16,8192]{2,0,1:T(1,128)S(1)}, u32[]{:S(2)}, u32[]{:S(2)}) async-start(f32[1,16,8192]{2,0,1:T(1,128)} %broadcast_in_dim.55), calls=%async_computation | async-start | bytes 1048576 | tf_op jit(solution)/shard_map/all_to_all | solution.py:51
  58.5 0.7 reduce_max.49
  59.2 0.7 fusion.14
  59.9 0.7 subtract_exponential_fusion
  60.6 12.1 %all-to-all-done = f32[1,16,8192]{2,0,1:T(1,128)S(1)} async-done(((f32[1,16,8192]{2,0,1:T(1,128)}), f32[1,16,8192]{2,0,1:T(1,128)S(1)}, u32[]{:S(2)}, u32[]{:S(2)}) %all-to-all-start) | async-done | bytes 524320 | tf_op jit(solution)/shard_map/all_to_all | solution.py:51
  72.7 0.2 mul.59
  72.9 0.8 %multiply_reduce_fusion = f32[8192]{0:T(1024)S(1)} fusion(f32[1,16,8192]{2,0,1:T(1,128)S(1)} %all-to-all-done, f32[1,16,8192]{2,0,1:T(1,128)S(1)} %bitcast.103), kind=kLoop, calls=%fused_computation.21 | loop fusion | flops 253952 | bytes 1081344 | tf_op jit(solution)/shard_map/reduce_sum | solution.py:58
  73.7 0.1 div.20
  73.7 0.7 divide_convert_fusion
  (11 shorter events, 0.1 us)
Async XLA Ops:
  3.3 25.4 %copy-start.1 = (bf16[1024,512]{1,0:T(8,128)(2,1)S(1)}, bf16[1024,512]{1,0:T(8,128)(2,1)}, u32[]{:S(2)}) copy-start(bf16[1024,512]{1,0:T(8,128)(2,1)} %param.10) | copy-start | bytes 3145732
  28.6 0.7 copy-start.6
  30.2 1.8 %copy-start.2 = (f32[16,16]{1,0:T(8,128)}, f32[16,16]{1,0:T(8,128)S(1)}, u32[]{:S(2)}) copy-start(f32[16,16]{1,0:T(8,128)S(1)} %get-tuple-element.11) | copy-start | bytes 3076
  32.0 0.7 copy-start.4
  32.6 10.5 %all-to-all-start.1 = ((f32[1,16,64]{2,0,1:T(1,128)}), f32[1,16,64]{2,0,1:T(1,128)}, u32[]{:S(2)}, u32[]{:S(2)}) async-start(f32[1,16,64]{2,0,1:T(1,128)} %bitcast.116), calls=%async_computation.1 | async-start | bytes 16384 | tf_op jit(solution)/shard_map/all_to_all | solution.py:52
  36.7 1.3 %copy-start.7 = (bf16[1,512]{1,0:T(2,128)(2,1)S(1)}, bf16[1,512]{1,0:T(2,128)(2,1)}, u32[]{:S(2)}) copy-start(bf16[1,512]{1,0:T(2,128)(2,1)} %param.9) | copy-start | bytes 3076
  38.1 0.7 copy-start.3
  39.2 1.3 %copy-start = (f32[16,16,1025]{2,1,0:T(8,128)S(1)}, f32[16,16,1025]{2,1,0:T(8,128)}, u32[]{:S(2)}) copy-start(f32[16,16,1025]{2,1,0:T(8,128)} %get-tuple-element.16) | copy-start | bytes 3148804
  39.2 1.3 %copy-start.5 = (f32[16,16]{1,0:T(8,128)S(1)}, f32[16,16]{1,0:T(8,128)}, u32[]{:S(2)}) copy-start(f32[16,16]{1,0:T(8,128)} %copy-done.4) | copy-start | bytes 3076
  43.2 11.7 %all-to-all-start.2 = ((f32[1,16,64]{2,0,1:T(1,128)}), f32[1,16,64]{2,0,1:T(1,128)S(1)}, u32[]{:S(2)}, u32[]{:S(2)}) async-start(f32[1,16,64]{2,0,1:T(1,128)} %bitcast.20), calls=%async_computation.2 | async-start | bytes 16384 | tf_op jit(solution)/shard_map/all_to_all | solution.py:53
  54.9 17.8 %all-to-all-start = ((f32[1,16,8192]{2,0,1:T(1,128)}), f32[1,16,8192]{2,0,1:T(1,128)S(1)}, u32[]{:S(2)}, u32[]{:S(2)}) async-start(f32[1,16,8192]{2,0,1:T(1,128)} %broadcast_in_dim.55), calls=%async_computation | async-start | bytes 1048576 | tf_op jit(solution)/shard_map/all_to_all | solution.py:51
where the time goes:
time: 75 us; the launch traced here: 74.4 us
  blocking collectives  24.9 us (33%)
  waiting for transfers between devices  17.6 us (23%)
  starting transfers between devices  13 us (17%)
  other arithmetic  7.23 us (10%)
  local copies, waits for them, and re-layouts  6.58 us (9%)
  matrix products  4.12 us (5%)
  between operations  0.93 us (1%)
    all_gather x1, blocking collectives, body(): gathered = lax.all_gather(queries, 'ctx', axis=0, tiled=True)  24.9 us
    all_to_all x1, waiting for transfers between devices, body(): lax.all_to_all(block_sum[None], 'ctx', split_axis=1, concat_axis=0, tiled...  12.1 us
    all_to_all x1, starting transfers between devices, body(): lax.all_to_all(block_total[None], 'ctx', split_axis=1, concat_axis=0, til...  5.35 us
    all_to_all x1, waiting for transfers between devices, body(): lax.all_to_all(block_total[None], 'ctx', split_axis=1, concat_axis=0, til...  4.99 us
    all_to_all x1, starting transfers between devices, body(): lax.all_to_all(block_max[None], 'ctx', split_axis=1, concat_axis=0, tiled...  4.08 us
    all_to_all x1, starting transfers between devices, body(): lax.all_to_all(block_sum[None], 'ctx', split_axis=1, concat_axis=0, tiled...  3.57 us
    unnamed x24, local copies, waits for them, and re-layouts  3.45 us
    dot_general x4, matrix products, body(): jnp.einsum('ngd,kd->ngk', query_part, key_part, preferred_element_type=jn...  2.63 us
  transfers between devices with their start and end apart: 3, of which 3 were waited for; matrix products, arithmetic and copies ran while one was open for 11% of the time, Pallas kernels for 0%

commit v1 on v0

--- a/solution.py
+++ b/solution.py
@@ -17,7 +17,28 @@
     query_heads = kv_heads * group_size
     all_keys = jnp.concatenate([cache_keys, fresh_keys], axis=0)
     all_values = jnp.concatenate([stored_values, fresh_values], axis=0)
-    gathered = lax.all_gather(queries, "ctx", axis=0, tiled=True)
+    later = lax.axis_index("ctx")
+    y = lax.axis_size("ctx")
+    arr_now, moved, taken_in = (y, later, queries.shape[0])
+    base_arr = jnp.zeros(
+        [i0 * arr_now if rr == 0 else i0 for rr, i0 in enumerate(queries.shape)], queries.dtype
+    )
+    gathered = lax.dynamic_update_slice_in_dim(base_arr, queries, moved * taken_in, axis=0)
+    z = raw_out = queries
+    for dev in range(1, arr_now // 2 + 1):
+        z = lax.ppermute(
+            z, axis_name="ctx", perm=[(rr, (rr + 1) % arr_now) for rr in range(arr_now)]
+        )
+        gathered = lax.dynamic_update_slice_in_dim(
+            gathered, z, (moved - dev) % arr_now * taken_in, axis=0
+        )
+        if 2 * dev < arr_now:
+            raw_out = lax.ppermute(
+                raw_out, "ctx", [(rr, (rr - 1) % arr_now) for rr in range(arr_now)]
+            )
+            gathered = lax.dynamic_update_slice_in_dim(
+                gathered, raw_out, (moved + dev) % arr_now * taken_in, axis=0
+            )
     total_new = gathered.shape[0]
     key_order = lax.dynamic_slice_in_dim(positions, device_rank * new_rows, new_rows, 0)
     live = jnp.arange(cache_rows, dtype=jnp.int32) < cache_lengths[0]

time: 75 us -> 99 us (1.32)
  starting transfers between devices: 13 us -> 45 us
  blocking collectives: 24.9 us -> 0 us
  waiting for transfers between devices: 17.6 us -> 31.6 us
  local copies, waits for them, and re-layouts: 6.58 us -> 12.2 us
  other arithmetic: 7.23 us -> 5.14 us
    ppermute x0 -> x15, starting transfers between devices: none -> 32.2 us  [the longest x7 31.7 us: body(): lax.ppermute(raw_out, 'ctx', [(rr, (rr - 1) % arr_now) for rr in range(ar...]
    all_gather x1 -> x0, blocking collectives: 24.9 us -> none  [body(): gathered = lax.all_gather(queries, 'ctx', axis=0, tiled=True)]
    dynamic_update_slice x0 -> x16, local copies, waits for them, and re-layouts: none -> 7.6 us  [the longest x8 3.8 us: body(): lax.dynamic_update_slice_in_dim(gathered, z, (moved - dev) % arr_now * ta...]
    ppermute x0 -> x15, waiting for transfers between devices: none -> 6.93 us  [the longest x7 6.39 us: body(): lax.ppermute(raw_out, 'ctx', [(rr, (rr - 1) % arr_now) for rr in range(ar...]
    all_to_all x1, waiting for transfers between devices: 0.56 us -> 5.5 us  [body(): lax.all_to_all(block_max[None], 'ctx', split_axis=1, concat_axis=0, tiled...]
    all_to_all x1, waiting for transfers between devices: 12.1 us -> 14.2 us  [body(): lax.all_to_all(block_sum[None], 'ctx', split_axis=1, concat_axis=0, tiled...]
    unnamed x24 -> x19, local copies, waits for them, and re-layouts: 3.45 us -> 1.46 us
    all_to_all x1, starting transfers between devices: 5.35 us -> 3.41 us  [body(): lax.all_to_all(block_total[None], 'ctx', split_axis=1, concat_axis=0, til...]
  transfers between devices with their start and end apart: 3 -> 18, of which waited for: 3 -> 9; matrix products, arithmetic and copies ran while one was open for 11% -> 14% of each run, Pallas kernels for 0% -> 0%
where the time goes in v1:
time: 99 us; the launch traced here: 98.6 us
  starting transfers between devices  45 us (45%)
  waiting for transfers between devices  31.6 us (32%)
  local copies, waits for them, and re-layouts  12.2 us (12%)
  other arithmetic  5.14 us (5%)
  matrix products  3.19 us (3%)
  between operations  1.46 us (1%)
    ppermute x7, starting transfers between devices, body(): lax.ppermute(raw_out, 'ctx', [(rr, (rr - 1) % arr_now) for rr in range(ar...  31.7 us
    all_to_all x1, waiting for transfers between devices, body(): lax.all_to_all(block_sum[None], 'ctx', split_axis=1, concat_axis=0, tiled...  14.2 us
    ppermute x7, waiting for transfers between devices, body(): lax.ppermute(raw_out, 'ctx', [(rr, (rr - 1) % arr_now) for rr in range(ar...  6.39 us
    all_to_all x1, starting transfers between devices, body(): lax.all_to_all(block_max[None], 'ctx', split_axis=1, concat_axis=0, tiled...  5.81 us
    all_to_all x1, waiting for transfers between devices, body(): lax.all_to_all(block_max[None], 'ctx', split_axis=1, concat_axis=0, tiled...  5.5 us
    all_to_all x1, waiting for transfers between devices, body(): lax.all_to_all(block_total[None], 'ctx', split_axis=1, concat_axis=0, til...  5.01 us
    dynamic_update_slice x8, local copies, waits for them, and re-layouts, body(): lax.dynamic_update_slice_in_dim(gathered, z, (moved - dev) % arr_now * ta...  3.8 us
    all_to_all x1, starting transfers between devices, body(): lax.all_to_all(block_sum[None], 'ctx', split_axis=1, concat_axis=0, tiled...  3.57 us
  transfers between devices with their start and end apart: 18, of which 9 were waited for; matrix products, arithmetic and copies ran while one was open for 14% of the time, Pallas kernels for 0%

profile of v1, /device:TPU:0, one launch (start us, length us, event | category | flops | bytes accessed | tf_op | source)
XLA Modules:
  0.0 98.6 jit_solution(16312736999738076978)
XLA Ops:
  0.0 0.5 collective-permute-start
  0.5 5.0 %collective-permute-start.1 = (bf16[1,8192]{1,0:T(2,128)(2,1)}, bf16[1,8192]{1,0:T(2,128)(2,1)S(1)}, u32[]{:S(2)}, u32[]{:S(2)}) collective-permute-start(bf16[1,8192]{1,0:T(2,128)(2,1)} %param.7), channel_id=1, source_target_pairs={{0,15},{1,0},{2,1},{3,2},{4,3},{5,4},{6,5},{7,6},{8,7},{9,8},{10,9... | collective-permute-start | bytes 49160 | tf_op jit(solution)/shard_map/ppermute | solution.py:36
  5.5 1.2 %dynamic_slice.3 = s32[1]{0:T(128)} dynamic-slice(s32[16]{0:T(128)} %param.13, s32[]{:T(128)S(6)} %select_n.125), dynamic_slice_sizes={1} | dynamic-slice | bytes 12 | tf_op jit(solution)/shard_map/dynamic_slice | solution.py:43
  6.7 0.5 collective-permute-done
  7.3 1.3 %compare_bitcast_fusion = pred[16,1]{0,1:T(4,128)(4,1)S(1)} fusion(s32[16]{0:T(128)} %param.13, s32[]{:T(128)} %bitcast.1), kind=kLoop, calls=%fused_computation.52 | loop fusion | flops 16 | bytes 84 | tf_op jit(solution)/shard_map/le | solution.py:46
  9.2 4.5 %collective-permute-start.3 = (bf16[1,8192]{1,0:T(2,128)(2,1)S(1)}, bf16[1,8192]{1,0:T(2,128)(2,1)S(1)}, u32[]{:S(2)}, u32[]{:S(2)}) collective-permute-start(bf16[1,8192]{1,0:T(2,128)(2,1)S(1)} %collective-permute-done.1), channel_id=1, source_target_pairs={{0,15},{1,0},{2,1},{3,2},{4,3},{5,4},{6,5},{7,6},{8,7},{9,8},{10,9... | collective-permute-start | bytes 49160 | tf_op jit(solution)/shard_map/ppermute | solution.py:36
  13.7 0.1 copy.9
  13.8 1.5 %collective-permute-done.3 = bf16[1,8192]{1,0:T(2,128)(2,1)S(1)} collective-permute-done((bf16[1,8192]{1,0:T(2,128)(2,1)S(1)}, bf16[1,8192]{1,0:T(2,128)(2,1)S(1)}, u32[]{:S(2)}, u32[]{:S(2)}) %collective-permute-start.3) | collective-permute-done | bytes 16416 | tf_op jit(solution)/shard_map/ppermute | solution.py:36
  15.3 4.5 %collective-permute-start.5 = (bf16[1,8192]{1,0:T(2,128)(2,1)S(1)}, bf16[1,8192]{1,0:T(2,128)(2,1)S(1)}, u32[]{:S(2)}, u32[]{:S(2)}) collective-permute-start(bf16[1,8192]{1,0:T(2,128)(2,1)S(1)} %collective-permute-done.3), channel_id=1, source_target_pairs={{0,15},{1,0},{2,1},{3,2},{4,3},{5,4},{6,5},{7,6},{8,7},{9,8},{10,9... | collective-permute-start | bytes 49160 | tf_op jit(solution)/shard_map/ppermute | solution.py:36
  19.8 1.6 %collective-permute-done.5 = bf16[1,8192]{1,0:T(2,128)(2,1)S(1)} collective-permute-done((bf16[1,8192]{1,0:T(2,128)(2,1)S(1)}, bf16[1,8192]{1,0:T(2,128)(2,1)S(1)}, u32[]{:S(2)}, u32[]{:S(2)}) %collective-permute-start.5) | collective-permute-done | bytes 16416 | tf_op jit(solution)/shard_map/ppermute | solution.py:36
  21.4 4.4 %collective-permute-start.7 = (bf16[1,8192]{1,0:T(2,128)(2,1)S(1)}, bf16[1,8192]{1,0:T(2,128)(2,1)S(1)}, u32[]{:S(2)}, u32[]{:S(2)}) collective-permute-start(bf16[1,8192]{1,0:T(2,128)(2,1)S(1)} %collective-permute-done.5), channel_id=1, source_target_pairs={{0,15},{1,0},{2,1},{3,2},{4,3},{5,4},{6,5},{7,6},{8,7},{9,8},{10,9... | collective-permute-start | bytes 49160 | tf_op jit(solution)/shard_map/ppermute | solution.py:36
  25.8 1.3 %constant_dynamic-update-slice_fusion.1 = bf16[1025,512]{1,0:T(8,128)(2,1)S(1)} fusion(bf16[1024,512]{1,0:T(8,128)(2,1)} %param.10), kind=kLoop, calls=%fused_computation.41 | loop fusion | bytes 2097152
  27.1 0.0 copy-start.4
  27.1 0.0 copy-start.5
  27.2 0.0 copy-start.1
  27.2 0.3 collective-permute-done.7
  27.4 4.4 %collective-permute-start.9 = (bf16[1,8192]{1,0:T(2,128)(2,1)S(1)}, bf16[1,8192]{1,0:T(2,128)(2,1)S(1)}, u32[]{:S(2)}, u32[]{:S(2)}) collective-permute-start(bf16[1,8192]{1,0:T(2,128)(2,1)S(1)} %collective-permute-done.7), channel_id=1, source_target_pairs={{0,15},{1,0},{2,1},{3,2},{4,3},{5,4},{6,5},{7,6},{8,7},{9,8},{10,9... | collective-permute-start | bytes 49160 | tf_op jit(solution)/shard_map/ppermute | solution.py:36
  31.9 0.1 constant_dynamic-update-slice_fusion.3
  31.9 1.5 %collective-permute-done.9 = bf16[1,8192]{1,0:T(2,128)(2,1)S(1)} collective-permute-done((bf16[1,8192]{1,0:T(2,128)(2,1)S(1)}, bf16[1,8192]{1,0:T(2,128)(2,1)S(1)}, u32[]{:S(2)}, u32[]{:S(2)}) %collective-permute-start.9) | collective-permute-done | bytes 16416 | tf_op jit(solution)/shard_map/ppermute | solution.py:36
  33.5 4.4 %collective-permute-start.11 = (bf16[1,8192]{1,0:T(2,128)(2,1)S(1)}, bf16[1,8192]{1,0:T(2,128)(2,1)S(1)}, u32[]{:S(2)}, u32[]{:S(2)}) collective-permute-start(bf16[1,8192]{1,0:T(2,128)(2,1)S(1)} %collective-permute-done.9), channel_id=1, source_target_pairs={{0,15},{1,0},{2,1},{3,2},{4,3},{5,4},{6,5},{7,6},{8,7},{9,8},{10,9... | collective-permute-start | bytes 49160 | tf_op jit(solution)/shard_map/ppermute | solution.py:36
  37.9 1.6 %collective-permute-done.11 = bf16[1,8192]{1,0:T(2,128)(2,1)S(1)} collective-permute-done((bf16[1,8192]{1,0:T(2,128)(2,1)S(1)}, bf16[1,8192]{1,0:T(2,128)(2,1)S(1)}, u32[]{:S(2)}, u32[]{:S(2)}) %collective-permute-start.11) | collective-permute-done | bytes 16416 | tf_op jit(solution)/shard_map/ppermute | solution.py:36
  39.5 4.4 %collective-permute-start.13 = (bf16[1,8192]{1,0:T(2,128)(2,1)S(1)}, bf16[1,8192]{1,0:T(2,128)(2,1)S(1)}, u32[]{:S(2)}, u32[]{:S(2)}) collective-permute-start(bf16[1,8192]{1,0:T(2,128)(2,1)S(1)} %collective-permute-done.11), channel_id=1, source_target_pairs={{0,15},{1,0},{2,1},{3,2},{4,3},{5,4},{6,5},{7,6},{8,7},{9,8},{10,9... | collective-permute-start | bytes 49160 | tf_op jit(solution)/shard_map/ppermute | solution.py:36
  43.9 0.0 collective-permute-done.12
  44.3 0.5 dynamic_update_slice.48
  44.9 0.5 dynamic_update_slice.49
  45.3 0.5 dynamic_update_slice.50
  45.8 0.5 dynamic_update_slice.51
  46.3 0.5 dynamic_update_slice.52
  46.8 0.5 dynamic_update_slice.53
  47.3 0.5 dynamic_update_slice.54
  47.8 0.5 dynamic_update_slice.55
  48.2 0.5 dynamic_update_slice.56
  48.7 0.5 dynamic_update_slice.57
  49.2 0.5 dynamic_update_slice.58
  49.7 0.5 dynamic_update_slice.59
  50.2 0.5 dynamic_update_slice.60
  50.7 0.5 dynamic_update_slice.61
  51.2 0.5 dynamic_update_slice.62
  51.7 0.5 dynamic_update_slice.63
  52.2 0.4 fusion.11
  52.6 0.4 fusion.12
  53.1 0.4 fusion.4
  53.4 0.5 convert_reduce_fusion
  53.9 0.4 fusion.5
  54.3 0.4 fusion.13
  54.8 0.4 fusion.14
  55.2 0.7 pad_maximum_fusion.1
  55.9 0.4 fusion.7
  56.3 0.5 convert_reduce_fusion.2
  56.7 0.4 fusion.6
  57.1 5.8 %all-to-all-start.1 = ((f32[1,16,64]{2,0,1:T(1,128)}), f32[1,16,64]{2,0,1:T(1,128)S(1)}, u32[]{:S(2)}, u32[]{:S(2)}) async-start(f32[1,16,64]{2,0,1:T(1,128)} %bitcast.11), calls=%async_computation.1 | async-start | bytes 16384 | tf_op jit(solution)/shard_map/all_to_all | solution.py:73
  62.9 0.1 copy_bitcast_fusion
  63.0 0.1 copy_bitcast_fusion.2
  63.1 0.7 pad_maximum_fusion.2
  63.8 5.5 %all-to-all-done.1 = f32[1,16,64]{2,0,1:T(1,128)S(1)} async-done(((f32[1,16,64]{2,0,1:T(1,128)}), f32[1,16,64]{2,0,1:T(1,128)S(1)}, u32[]{:S(2)}, u32[]{:S(2)}) %all-to-all-start.1) | async-done | bytes 4128 | tf_op jit(solution)/shard_map/all_to_all | solution.py:73
  69.3 3.4 %all-to-all-start.2 = ((f32[1,16,64]{2,0,1:T(1,128)}), f32[1,16,64]{2,0,1:T(1,128)S(1)}, u32[]{:S(2)}, u32[]{:S(2)}) async-start(f32[1,16,64]{2,0,1:T(1,128)} %bitcast.15), calls=%async_computation.2 | async-start | bytes 16384 | tf_op jit(solution)/shard_map/all_to_all | solution.py:74
  72.8 1.3 %broadcast_in_dim.59 = f32[1,16,8192]{2,0,1:T(1,128)} reshape(f32[16,8192]{1,0:T(8,128)S(1)} %pad_maximum_fusion) | data formatting | bytes 1048576 | tf_op jit(solution)/shard_map/broadcast_in_dim | solution.py:72
  74.1 5.0 %all-to-all-done.2 = f32[1,16,64]{2,0,1:T(1,128)S(1)} async-done(((f32[1,16,64]{2,0,1:T(1,128)}), f32[1,16,64]{2,0,1:T(1,128)S(1)}, u32[]{:S(2)}, u32[]{:S(2)}) %all-to-all-start.2) | async-done | bytes 4128 | tf_op jit(solution)/shard_map/all_to_all | solution.py:74
  79.1 3.6 %all-to-all-start = ((f32[1,16,8192]{2,0,1:T(1,128)}), f32[1,16,8192]{2,0,1:T(1,128)S(1)}, u32[]{:S(2)}, u32[]{:S(2)}) async-start(f32[1,16,8192]{2,0,1:T(1,128)} %broadcast_in_dim.59), calls=%async_computation | async-start | bytes 1048576 | tf_op jit(solution)/shard_map/all_to_all | solution.py:72
  82.8 14.2 %all-to-all-done = f32[1,16,8192]{2,0,1:T(1,128)S(1)} async-done(((f32[1,16,8192]{2,0,1:T(1,128)}), f32[1,16,8192]{2,0,1:T(1,128)S(1)}, u32[]{:S(2)}, u32[]{:S(2)}) %all-to-all-start) | async-done | bytes 524320 | tf_op jit(solution)/shard_map/all_to_all | solution.py:72
  96.9 0.2 mul.43
  97.1 0.8 multiply_reduce_fusion
  97.9 0.1 div.20
  98.0 0.7 divide_convert_fusion
  (39 shorter events, 0.3 us)
Async XLA Ops:
  0.0 31.9 %copy-start = (bf16[1024,512]{1,0:T(8,128)(2,1)S(1)}, bf16[1024,512]{1,0:T(8,128)(2,1)}, u32[]{:S(2)}) copy-start(bf16[1024,512]{1,0:T(8,128)(2,1)} %param.11) | copy-start | bytes 3145732
  0.0 7.3 %collective-permute-start = (bf16[1,8192]{1,0:T(2,128)(2,1)}, bf16[1,8192]{1,0:T(2,128)(2,1)S(1)}, u32[]{:S(2)}, u32[]{:S(2)}) collective-permute-start(bf16[1,8192]{1,0:T(2,128)(2,1)} %param.7), channel_id=1, source_target_pairs={{0,1},{1,2},{2,3},{3,4},{4,5},{5,6},{6,7},{7,8},{8,9},{9,10},{10,1... | collective-permute-start | bytes 49160 | tf_op jit(solution)/shard_map/ppermute | solution.py:29
  0.5 8.7 %collective-permute-start.1 = (bf16[1,8192]{1,0:T(2,128)(2,1)}, bf16[1,8192]{1,0:T(2,128)(2,1)S(1)}, u32[]{:S(2)}, u32[]{:S(2)}) collective-permute-start(bf16[1,8192]{1,0:T(2,128)(2,1)} %param.7), channel_id=1, source_target_pairs={{0,15},{1,0},{2,1},{3,2},{4,3},{5,4},{6,5},{7,6},{8,7},{9,8},{10,9... | collective-permute-start | bytes 49160 | tf_op jit(solution)/shard_map/ppermute | solution.py:36
  7.3 6.5 %collective-permute-start.2 = (bf16[1,8192]{1,0:T(2,128)(2,1)S(1)}, bf16[1,8192]{1,0:T(2,128)(2,1)S(1)}, u32[]{:S(2)}, u32[]{:S(2)}) collective-permute-start(bf16[1,8192]{1,0:T(2,128)(2,1)S(1)} %collective-permute-done), channel_id=1, source_target_pairs={{0,1},{1,2},{2,3},{3,4},{4,5},{5,6},{6,7},{7,8},{8,9},{9,10},{10,1... | collective-permute-start | bytes 49160 | tf_op jit(solution)/shard_map/ppermute | solution.py:29
  9.2 6.1 %collective-permute-start.3 = (bf16[1,8192]{1,0:T(2,128)(2,1)S(1)}, bf16[1,8192]{1,0:T(2,128)(2,1)S(1)}, u32[]{:S(2)}, u32[]{:S(2)}) collective-permute-start(bf16[1,8192]{1,0:T(2,128)(2,1)S(1)} %collective-permute-done.1), channel_id=1, source_target_pairs={{0,15},{1,0},{2,1},{3,2},{4,3},{5,4},{6,5},{7,6},{8,7},{9,8},{10,9... | collective-permute-start | bytes 49160 | tf_op jit(solution)/shard_map/ppermute | solution.py:36
  13.7 6.1 %collective-permute-start.4 = (bf16[1,8192]{1,0:T(2,128)(2,1)S(1)}, bf16[1,8192]{1,0:T(2,128)(2,1)S(1)}, u32[]{:S(2)}, u32[]{:S(2)}) collective-permute-start(bf16[1,8192]{1,0:T(2,128)(2,1)S(1)} %collective-permute-done.2), channel_id=1, source_target_pairs={{0,1},{1,2},{2,3},{3,4},{4,5},{5,6},{6,7},{7,8},{8,9},{9,10},{10,1... | collective-permute-start | bytes 49160 | tf_op jit(solution)/shard_map/ppermute | solution.py:29
  15.3 6.1 %collective-permute-start.5 = (bf16[1,8192]{1,0:T(2,128)(2,1)S(1)}, bf16[1,8192]{1,0:T(2,128)(2,1)S(1)}, u32[]{:S(2)}, u32[]{:S(2)}) collective-permute-start(bf16[1,8192]{1,0:T(2,128)(2,1)S(1)} %collective-permute-done.3), channel_id=1, source_target_pairs={{0,15},{1,0},{2,1},{3,2},{4,3},{5,4},{6,5},{7,6},{8,7},{9,8},{10,9... | collective-permute-start | bytes 49160 | tf_op jit(solution)/shard_map/ppermute | solution.py:36
  19.8 6.0 %collective-permute-start.6 = (bf16[1,8192]{1,0:T(2,128)(2,1)S(1)}, bf16[1,8192]{1,0:T(2,128)(2,1)S(1)}, u32[]{:S(2)}, u32[]{:S(2)}) collective-permute-start(bf16[1,8192]{1,0:T(2,128)(2,1)S(1)} %collective-permute-done.4), channel_id=1, source_target_pairs={{0,1},{1,2},{2,3},{3,4},{4,5},{5,6},{6,7},{7,8},{8,9},{9,10},{10,1... | collective-permute-start | bytes 49160 | tf_op jit(solution)/shard_map/ppermute | solution.py:29
  21.4 6.0 %collective-permute-start.7 = (bf16[1,8192]{1,0:T(2,128)(2,1)S(1)}, bf16[1,8192]{1,0:T(2,128)(2,1)S(1)}, u32[]{:S(2)}, u32[]{:S(2)}) collective-permute-start(bf16[1,8192]{1,0:T(2,128)(2,1)S(1)} %collective-permute-done.5), channel_id=1, source_target_pairs={{0,15},{1,0},{2,1},{3,2},{4,3},{5,4},{6,5},{7,6},{8,7},{9,8},{10,9... | collective-permute-start | bytes 49160 | tf_op jit(solution)/shard_map/ppermute | solution.py:36
  25.8 6.0 %collective-permute-start.8 = (bf16[1,8192]{1,0:T(2,128)(2,1)S(1)}, bf16[1,8192]{1,0:T(2,128)(2,1)S(1)}, u32[]{:S(2)}, u32[]{:S(2)}) collective-permute-start(bf16[1,8192]{1,0:T(2,128)(2,1)S(1)} %collective-permute-done.6), channel_id=1, source_target_pairs={{0,1},{1,2},{2,3},{3,4},{4,5},{5,6},{6,7},{7,8},{8,9},{9,10},{10,1... | collective-permute-start | bytes 49160 | tf_op jit(solution)/shard_map/ppermute | solution.py:29
  27.1 10.8 %copy-start.4 = (bf16[1,512]{1,0:T(2,128)(2,1)S(1)}, bf16[1,512]{1,0:T(2,128)(2,1)}, u32[]{:S(2)}) copy-start(bf16[1,512]{1,0:T(2,128)(2,1)} %param.8) | copy-start | bytes 3076
  27.1 16.8 %copy-start.5 = (bf16[1,512]{1,0:T(2,128)(2,1)S(1)}, bf16[1,512]{1,0:T(2,128)(2,1)}, u32[]{:S(2)}) copy-start(bf16[1,512]{1,0:T(2,128)(2,1)} %param.9) | copy-start | bytes 3076
  27.2 17.1 %copy-start.1 = (bf16[1,8192]{1,0:T(2,128)(2,1)S(1)}, bf16[1,8192]{1,0:T(2,128)(2,1)}, u32[]{:S(2)}) copy-start(bf16[1,8192]{1,0:T(2,128)(2,1)} %param.7) | copy-start | bytes 49156
  27.4 6.0 %collective-permute-start.9 = (bf16[1,8192]{1,0:T(2,128)(2,1)S(1)}, bf16[1,8192]{1,0:T(2,128)(2,1)S(1)}, u32[]{:S(2)}, u32[]{:S(2)}) collective-permute-start(bf16[1,8192]{1,0:T(2,128)(2,1)S(1)} %collective-permute-done.7), channel_id=1, source_target_pairs={{0,15},{1,0},{2,1},{3,2},{4,3},{5,4},{6,5},{7,6},{8,7},{9,8},{10,9... | collective-permute-start | bytes 49160 | tf_op jit(solution)/shard_map/ppermute | solution.py:36
  31.9 6.0 %collective-permute-start.10 = (bf16[1,8192]{1,0:T(2,128)(2,1)S(1)}, bf16[1,8192]{1,0:T(2,128)(2,1)S(1)}, u32[]{:S(2)}, u32[]{:S(2)}) collective-permute-start(bf16[1,8192]{1,0:T(2,128)(2,1)S(1)} %collective-permute-done.8), channel_id=1, source_target_pairs={{0,1},{1,2},{2,3},{3,4},{4,5},{5,6},{6,7},{7,8},{8,9},{9,10},{10,1... | collective-permute-start | bytes 49160 | tf_op jit(solution)/shard_map/ppermute | solution.py:29
  33.5 6.0 %collective-permute-start.11 = (bf16[1,8192]{1,0:T(2,128)(2,1)S(1)}, bf16[1,8192]{1,0:T(2,128)(2,1)S(1)}, u32[]{:S(2)}, u32[]{:S(2)}) collective-permute-start(bf16[1,8192]{1,0:T(2,128)(2,1)S(1)} %collective-permute-done.9), channel_id=1, source_target_pairs={{0,15},{1,0},{2,1},{3,2},{4,3},{5,4},{6,5},{7,6},{8,7},{9,8},{10,9... | collective-permute-start | bytes 49160 | tf_op jit(solution)/shard_map/ppermute | solution.py:36
  37.9 6.0 %copy-start.2 = (bf16[1,8192]{1,0:T(2,128)(2,1)}, bf16[1,8192]{1,0:T(2,128)(2,1)S(1)}, u32[]{:S(2)}) copy-start(bf16[1,8192]{1,0:T(2,128)(2,1)S(1)} %collective-permute-done.10) | copy-start | bytes 49156
  37.9 6.0 %collective-permute-start.12 = (bf16[1,8192]{1,0:T(2,128)(2,1)S(1)}, bf16[1,8192]{1,0:T(2,128)(2,1)S(1)}, u32[]{:S(2)}, u32[]{:S(2)}) collective-permute-start(bf16[1,8192]{1,0:T(2,128)(2,1)S(1)} %collective-permute-done.10), channel_id=1, source_target_pairs={{0,1},{1,2},{2,3},{3,4},{4,5},{5,6},{6,7},{7,8},{8,9},{9,10},{10,1... | collective-permute-start | bytes 49160 | tf_op jit(solution)/shard_map/ppermute | solution.py:29
  39.5 11.7 %collective-permute-start.13 = (bf16[1,8192]{1,0:T(2,128)(2,1)S(1)}, bf16[1,8192]{1,0:T(2,128)(2,1)S(1)}, u32[]{:S(2)}, u32[]{:S(2)}) collective-permute-start(bf16[1,8192]{1,0:T(2,128)(2,1)S(1)} %collective-permute-done.11), channel_id=1, source_target_pairs={{0,15},{1,0},{2,1},{3,2},{4,3},{5,4},{6,5},{7,6},{8,7},{9,8},{10,9... | collective-permute-start | bytes 49160 | tf_op jit(solution)/shard_map/ppermute | solution.py:36
  43.9 7.7 %collective-permute-start.14 = (bf16[1,8192]{1,0:T(2,128)(2,1)S(1)}, bf16[1,8192]{1,0:T(2,128)(2,1)S(1)}, u32[]{:S(2)}, u32[]{:S(2)}) collective-permute-start(bf16[1,8192]{1,0:T(2,128)(2,1)S(1)} %collective-permute-done.12), channel_id=1, source_target_pairs={{0,1},{1,2},{2,3},{3,4},{4,5},{5,6},{6,7},{7,8},{8,9},{9,10},{10,1... | collective-permute-start | bytes 49160 | tf_op jit(solution)/shard_map/ppermute | solution.py:29
  44.0 5.7 %copy-start.3 = (bf16[1,8192]{1,0:T(2,128)(2,1)S(1)}, bf16[1,8192]{1,0:T(2,128)(2,1)}, u32[]{:S(2)}) copy-start(bf16[1,8192]{1,0:T(2,128)(2,1)} %copy-done.2) | copy-start | bytes 49156
  57.1 12.2 %all-to-all-start.1 = ((f32[1,16,64]{2,0,1:T(1,128)}), f32[1,16,64]{2,0,1:T(1,128)S(1)}, u32[]{:S(2)}, u32[]{:S(2)}) async-start(f32[1,16,64]{2,0,1:T(1,128)} %bitcast.11), calls=%async_computation.1 | async-start | bytes 16384 | tf_op jit(solution)/shard_map/all_to_all | solution.py:73
  69.3 9.8 %all-to-all-start.2 = ((f32[1,16,64]{2,0,1:T(1,128)}), f32[1,16,64]{2,0,1:T(1,128)S(1)}, u32[]{:S(2)}, u32[]{:S(2)}) async-start(f32[1,16,64]{2,0,1:T(1,128)} %bitcast.15), calls=%async_computation.2 | async-start | bytes 16384 | tf_op jit(solution)/shard_map/all_to_all | solution.py:74
  79.1 17.8 %all-to-all-start = ((f32[1,16,8192]{2,0,1:T(1,128)}), f32[1,16,8192]{2,0,1:T(1,128)S(1)}, u32[]{:S(2)}, u32[]{:S(2)}) async-start(f32[1,16,8192]{2,0,1:T(1,128)} %broadcast_in_dim.59), calls=%async_computation | async-start | bytes 1048576 | tf_op jit(solution)/shard_map/all_to_all | solution.py:72
